TPU v7x, 32 devices: a whole 2x2x4 slice. The times are simulated.
32 devices in a mesh: ctx: 16 (over z, y, core), head: 2 (over x).
Axes of the slice: x: 2, y: 2, z: 4, core: 2. Of those that a mesh axis runs over, the one named last changes fastest.
Arguments:
- fine_query: bfloat16 [4096, 4096], P('ctx', 'head'), may hold values from -181 to 181
- fine_memory: bfloat16 [2, 4096, 1024], P(None, 'ctx', 'head'), may hold values from -6.5 to 6.5
- coarse_query: bfloat16 [2048, 4096], P('ctx', 'head'), may hold values from -181 to 181
- coarse_memory: bfloat16 [2, 2048, 1024], P(None, 'ctx', 'head'), may hold values from -6.5 to 6.5
- coarse_scale: int32 [2048], P('ctx'), may hold values from 0 to 7, never falling along the last dimension, each value on 1 to 512 neighbouring positions
- out_weight: bfloat16 [4096, 4096], P('head'), may hold values from -0.09375 to 0.09375
Outputs:
- fine_mixed: bfloat16 [4096, 4096], P(('ctx', 'head'))
- coarse_mixed: bfloat16 [2048, 4096], P(('ctx', 'head'))
Inputs may be any that keep to these rules, and one draw needn't show every extreme that they name: `coarse_scale`: never falls along the coarse tokens.
All inputs are finite; a program needn't handle non-finite values.
Results may differ from a plain program's by a relative error of at most 0.014.
Values may be sent and summed in bfloat16 or wider, within the bound.
A program may use at most 128 MiB of HBM per device.

v0:
```python
import math

import jax
import jax.numpy as jnp
from jax import lax
from jax.sharding import PartitionSpec as P

HD = 128


masked_score = -1e30


def attend_block(running, grouped, key_block, value_block, allowed, factor):
    running_max, running_sum, weighted = running
    scores = (
        jnp.einsum("rkgd,pkd->kgrp", grouped, key_block, preferred_element_type=jnp.float32)
        * factor
    )
    if allowed is not None:
        scores = jnp.where(allowed[None, None], scores, masked_score)
    new_max = jnp.maximum(running_max, jnp.max(scores, axis=-1))
    rescale = jnp.exp(running_max - new_max)
    shifted = jnp.exp(scores - new_max[..., None])
    running_sum = running_sum * rescale + jnp.sum(shifted, axis=-1)
    weighted = weighted * rescale[..., None] + jnp.einsum(
        "kgrp,pkd->kgrd",
        shifted.astype(jnp.bfloat16),
        value_block,
        preferred_element_type=jnp.float32,
    )
    return (new_max, running_sum, weighted)


def fold_keys(running, grouped, kv_piece, key_level, query_level, factor):
    length = kv_piece.shape[1]
    span_rows = math.gcd(length, 1024)
    block_count = length // span_rows
    groups = grouped.shape[1]
    key_blocks = kv_piece[0].reshape(block_count, span_rows, groups, -1)
    value_blocks = kv_piece[1].reshape(block_count, span_rows, groups, -1)
    if key_level is None:

        def advance(state, pieces):
            return (attend_block(state, grouped, pieces[0], pieces[1], None, factor), None)

        result, unused = lax.scan(advance, running, (key_blocks, value_blocks))
    else:
        level_blocks = key_level.reshape(block_count, span_rows)

        def advance(state, pieces):
            allowed = pieces[2][None, :] <= query_level[:, None]
            return (attend_block(state, grouped, pieces[0], pieces[1], allowed, factor), None)

        result, unused = lax.scan(advance, running, (key_blocks, value_blocks, level_blocks))
    return result


def mix_rows(attention, out_weight):
    return jnp.dot(attention, out_weight, preferred_element_type=jnp.float32)


def per_device(fine_query, fine_memory, coarse_query, coarse_memory, coarse_scale, out_weight):
    factor = HD ** (-0.5)
    groups = fine_memory.shape[2] // HD
    ratio = fine_query.shape[1] // (groups * HD)
    fine_rows = fine_query.shape[0]
    coarse_rows = coarse_query.shape[0]

    def group_rows(query):
        return query.reshape(query.shape[0], groups, ratio, HD)

    def start_state(length):
        return (
            jnp.full((groups, ratio, length), masked_score, jnp.float32),
            jnp.zeros((groups, ratio, length), jnp.float32),
            jnp.zeros((groups, ratio, length, HD), jnp.float32),
        )

    def finish(state):
        result = state[2] / state[1][..., None]
        return result.transpose(2, 0, 1, 3).reshape(result.shape[2], -1).astype(jnp.bfloat16)

    coarse_levels = coarse_scale.astype(jnp.float32)
    fine_grouped = group_rows(fine_query)
    fine_state = fold_keys(
        start_state(fine_rows),
        fine_grouped,
        lax.all_gather(fine_memory, "ctx", axis=1, tiled=True),
        None,
        None,
        factor,
    )
    whole_memory, whole_levels = (
        lax.all_gather(coarse_memory, "ctx", axis=1, tiled=True),
        lax.all_gather(
            coarse_levels.astype(jnp.bfloat16).reshape(1, -1), "ctx", axis=1, tiled=True
        ),
    )
    fine_state = fold_keys(fine_state, fine_grouped, whole_memory, None, None, factor)
    coarse_state = fold_keys(
        start_state(coarse_rows),
        group_rows(coarse_query),
        whole_memory,
        whole_levels[0].astype(jnp.float32),
        coarse_levels,
        factor,
    )
    fine_attention = finish(fine_state)
    coarse_attention = finish(coarse_state)
    fine_mixed = lax.psum_scatter(
        mix_rows(fine_attention, out_weight).astype(jnp.bfloat16),
        "head",
        scatter_dimension=0,
        tiled=True,
    )
    coarse_mixed = lax.psum_scatter(
        mix_rows(coarse_attention, out_weight).astype(jnp.bfloat16),
        "head",
        scatter_dimension=0,
        tiled=True,
    )
    return (fine_mixed, coarse_mixed)


def solution(mesh):
    placed = (
        P("ctx", "head"),
        P(None, "ctx", "head"),
        P("ctx", "head"),
        P(None, "ctx", "head"),
        P("ctx"),
        P("head", None),
    )
    return jax.shard_map(
        per_device,
        mesh=mesh,
        in_specs=placed,
        out_specs=(P(("ctx", "head"), None), P(("ctx", "head"), None)),
        check_vma=False,
    )
```

profile of v0, /device:TPU:0, one launch (start us, length us, event | category | flops | bytes accessed | tf_op | source)
XLA Modules:
  0.0 370.5 jit_solution(7867573203565260531)
XLA Ops:
  13.3 23.1 %all-gather.1 = bf16[16,1,128]{2,1,0:T(2,128)(2,1)S(1)} all-gather(bf16[1,1,128]{2,1,0:T(2,128)(2,1)S(1)} %get-tuple-element.299), channel_id=2, replica_groups=mesh['ctx'=16,'head'=2] {'ctx'}, dimensions={0}, use_global_device_ids=true | all-gather | bytes 4352 | tf_op jit(solution)/shard_map/all_gather | solution.py:96
  40.6 22.8 %all-gather.7.cloned.1.call-done = bf16[2,2048,512]{2,1,0:T(8,128)(2,1)} async-done(((bf16[2,128,512]{2,1,0:T(8,128)(2,1)}), bf16[2,2048,512]{2,1,0:T(8,128)(2,1)}) %all-gather.7.cloned.1.call-update) | async-done | bytes 4194320 | tf_op jit(solution)/shard_map/all_gather | solution.py:95
  82.3 33.2 %while.46 = (s32[]{:T(128)}, f32[4,4,128]{2,1,0:T(4,128)S(1)}, f32[4,4,128]{2,1,0:T(4,128)S(1)}, f32[4,4,128,128]{3,2,1,0:T(8,128)}, f32[2,1024]{1,0:T(2,128)S(1...) while((s32[]{:T(128)}, f32[4,4,128]{2,1,0:T(4,128)S(1)}, ...), condition=%wide.region_12.13_spmd.clone, body=%wide.region_9.12_spmd.clone.sunk | while | flops 1097738240 | bytes 64108184 | solution.py:55
  119.4 9.5 %convolution_convert_fusion.1 = bf16[128,4096]{1,0:T(8,128)(2,1)} fusion(bf16[128,2048]{0,1:T(8,128)(2,1)S(1)} %bitcast.155, bf16[2048,4096]{1,0:T(8,128)(2,1)} %param.17), kind=kOutput, calls=%fused_computation.64 | convolution fusion | flops 2148007936 | bytes 18350080 | tf_op jit(solution)/shard_map/dot_general | solution.py:60
  129.2 9.2 %all-gather.5.cloned.1.call-done = bf16[2,4096,512]{2,1,0:T(8,128)(2,1)} async-done(((bf16[2,256,512]{2,1,0:T(8,128)(2,1)}), bf16[2,4096,512]{2,1,0:T(8,128)(2,1)}) %all-gather.5.cloned.1.call-update) | async-done | bytes 8388624 | tf_op jit(solution)/shard_map/all_gather | solution.py:89
  158.0 107.8 %while.45 = (s32[]{:T(128)}, f32[4,4,256]{2,1,0:T(4,128)S(1)}, f32[4,4,256]{2,1,0:T(4,128)S(1)}, f32[4,4,256,128]{3,2,1,0:T(8,128)S(1)}, bf16[4,1024,4,128]{3,2,...) while((s32[]{:T(128)}, f32[4,4,256]{2,1,0:T(4,128)S(1)}, ...), condition=%wide.region_3.4_spmd.clone, body=%wide.region_0.3_spmd.clone.sunk | while | flops 2182631424 | bytes 66322564 | solution.py:47
  168.2 8.7 %fusion.81 = f32[4,4,256]{2,1,0:T(4,128)S(1)} fusion(f32[4,1024,256,4]{2,1,3,0:T(8,128)} %get-tuple-element.456, f32[4,4,256]{2,1,0:T(4,128)S(1)} %select_maximum_fusion.4), kind=kLoop, calls=%fused_computation.23.clone.1 | loop fusion | flops 12578816 | bytes 16809984 | tf_op jit(solution)/shard_map/while/body/eval_jaxpr/reduce_sum | solution.py:25
  176.9 8.0 %fusion.83 = f32[4,4,256,128]{3,2,1,0:T(8,128)S(1)} fusion(f32[4,4,256,128]{3,2,1,0:T(8,128)S(1)} %get-tuple-element.485, f32[4,1024,256,4]{2,1,3,0:T(8,128)} %get-tuple-element.456, f32[4,4,256]{2,1,0:T(4,128)S(1)} %select_maximum_fusion.4, bf16[1,1024,4,128]{3,2,1,0:T(4,128)(2,1)S(1)} %copy-done.1, f32[4,4,256]{2,1,0:T(4,128)S(1)} %get-tuple-element.459, ...), kind=kOutput, calls=%fused_computation.28.clone.1 | convolution fusion | flops 1087897600 | bytes 22052864 | tf_op jit(solution)/shard_map/while/body/eval_jaxpr/kgrp,pkd->kgrd/dot_general | solution.py:26
  195.2 8.7 %fusion.81 = f32[4,4,256]{2,1,0:T(4,128)S(1)} fusion(f32[4,1024,256,4]{2,1,3,0:T(8,128)} %get-tuple-element.456, f32[4,4,256]{2,1,0:T(4,128)S(1)} %select_maximum_fusion.4), kind=kLoop, calls=%fused_computation.23.clone.1 | loop fusion | flops 12578816 | bytes 16809984 | tf_op jit(solution)/shard_map/while/body/eval_jaxpr/reduce_sum | solution.py:25
  203.9 8.0 %fusion.83 = f32[4,4,256,128]{3,2,1,0:T(8,128)S(1)} fusion(f32[4,4,256,128]{3,2,1,0:T(8,128)S(1)} %get-tuple-element.485, f32[4,1024,256,4]{2,1,3,0:T(8,128)} %get-tuple-element.456, f32[4,4,256]{2,1,0:T(4,128)S(1)} %select_maximum_fusion.4, bf16[1,1024,4,128]{3,2,1,0:T(4,128)(2,1)S(1)} %copy-done.1, f32[4,4,256]{2,1,0:T(4,128)S(1)} %get-tuple-element.459, ...), kind=kOutput, calls=%fused_computation.28.clone.1 | convolution fusion | flops 1087897600 | bytes 22052864 | tf_op jit(solution)/shard_map/while/body/eval_jaxpr/kgrp,pkd->kgrd/dot_general | solution.py:26
  215.1 7.0 %bitcast_reduce_fusion.5 = (f32[4,4,256]{2,1,0:T(4,128)S(1)}, f32[4,1024,256,4]{2,1,3,0:T(8,128)}) fusion(bf16[256,4,4,128]{3,0,2,1:T(8,128)(2,1)S(1)} %get-tuple-element.496, bf16[1,1024,4,128]{3,2,1,0:T(4,128)(2,1)S(1)} %get-tuple-element.454), kind=kOutput, calls=%fused_computation.20.clone.1 | convolution fusion | flops 1082126336 | bytes 18890752 | tf_op jit(solution)/shard_map/while/body/eval_jaxpr/rkgd,pkd->kgrp/dot_general | solution.py:17
  222.1 8.7 %fusion.81 = f32[4,4,256]{2,1,0:T(4,128)S(1)} fusion(f32[4,1024,256,4]{2,1,3,0:T(8,128)} %get-tuple-element.456, f32[4,4,256]{2,1,0:T(4,128)S(1)} %select_maximum_fusion.4), kind=kLoop, calls=%fused_computation.23.clone.1 | loop fusion | flops 12578816 | bytes 16809984 | tf_op jit(solution)/shard_map/while/body/eval_jaxpr/reduce_sum | solution.py:25
  230.8 8.0 %fusion.83 = f32[4,4,256,128]{3,2,1,0:T(8,128)S(1)} fusion(f32[4,4,256,128]{3,2,1,0:T(8,128)S(1)} %get-tuple-element.485, f32[4,1024,256,4]{2,1,3,0:T(8,128)} %get-tuple-element.456, f32[4,4,256]{2,1,0:T(4,128)S(1)} %select_maximum_fusion.4, bf16[1,1024,4,128]{3,2,1,0:T(4,128)(2,1)S(1)} %copy-done.1, f32[4,4,256]{2,1,0:T(4,128)S(1)} %get-tuple-element.459, ...), kind=kOutput, calls=%fused_computation.28.clone.1 | convolution fusion | flops 1087897600 | bytes 22052864 | tf_op jit(solution)/shard_map/while/body/eval_jaxpr/kgrp,pkd->kgrd/dot_general | solution.py:26
  249.1 8.7 %fusion.81 = f32[4,4,256]{2,1,0:T(4,128)S(1)} fusion(f32[4,1024,256,4]{2,1,3,0:T(8,128)} %get-tuple-element.456, f32[4,4,256]{2,1,0:T(4,128)S(1)} %select_maximum_fusion.4), kind=kLoop, calls=%fused_computation.23.clone.1 | loop fusion | flops 12578816 | bytes 16809984 | tf_op jit(solution)/shard_map/while/body/eval_jaxpr/reduce_sum | solution.py:25
  257.8 8.0 %fusion.83 = f32[4,4,256,128]{3,2,1,0:T(8,128)S(1)} fusion(f32[4,4,256,128]{3,2,1,0:T(8,128)S(1)} %get-tuple-element.485, f32[4,1024,256,4]{2,1,3,0:T(8,128)} %get-tuple-element.456, f32[4,4,256]{2,1,0:T(4,128)S(1)} %select_maximum_fusion.4, bf16[1,1024,4,128]{3,2,1,0:T(4,128)(2,1)S(1)} %copy-done.1, f32[4,4,256]{2,1,0:T(4,128)S(1)} %get-tuple-element.459, ...), kind=kOutput, calls=%fused_computation.28.clone.1 | convolution fusion | flops 1087897600 | bytes 22052864 | tf_op jit(solution)/shard_map/while/body/eval_jaxpr/kgrp,pkd->kgrd/dot_general | solution.py:26
  265.8 52.2 %while.44 = (s32[]{:T(128)}, f32[4,4,256]{2,1,0:T(4,128)S(1)}, f32[4,4,256]{2,1,0:T(4,128)S(1)}, f32[4,4,256,128]{3,2,1,0:T(8,128)S(1)}, bf16[2,1024,4,128]{3,1,...) while((s32[]{:T(128)}, f32[4,4,256]{2,1,0:T(4,128)S(1)}, ...), condition=%wide.region_7.8_spmd, body=%wide.region_4.7_spmd.sunk | while | flops 2182094848 | bytes 66323060 | solution.py:47
  266.0 9.3 %bitcast_reduce_fusion.4 = (f32[4,4,256]{2,1,0:T(4,128)S(1)}, f32[4,1024,256,4]{2,1,3,0:T(8,128)}) fusion(bf16[256,4,4,128]{3,0,2,1:T(8,128)(2,1)S(1)} %get-tuple-element.521, bf16[2,1024,4,128]{3,1,2,0:T(8,128)(2,1)} %get-tuple-element.520, s32[]{:T(128)} %get-tuple-element.508), kind=kOutput, calls=%fused_computation.1.clone.1 | convolution fusion | flops 1082126336 | bytes 18891264 | tf_op jit(solution)/shard_map/while/body/eval_jaxpr/rkgd,pkd->kgrp/dot_general | solution.py:17
  275.3 8.7 %fusion.78 = f32[4,4,256]{2,1,0:T(4,128)S(1)} fusion(f32[4,1024,256,4]{2,1,3,0:T(8,128)} %get-tuple-element.444, f32[4,4,256]{2,1,0:T(4,128)S(1)} %max.16), kind=kLoop, calls=%fused_computation.4.clone.1 | loop fusion | flops 12578816 | bytes 16809984 | tf_op jit(solution)/shard_map/while/body/eval_jaxpr/reduce_sum | solution.py:25
  284.1 7.9 %multiply_add_fusion.5 = f32[4,4,256,128]{3,2,1,0:T(8,128)S(1)} fusion(f32[4,4,256,128]{3,2,1,0:T(8,128)S(1)} %get-tuple-element.511, f32[4,1024,256,4]{2,1,3,0:T(8,128)} %get-tuple-element.444, f32[4,4,256]{2,1,0:T(4,128)S(1)} %max.16, bf16[2,1024,4,128]{3,1,2,0:T(8,128)(2,1)S(1)} %copy-done.2, s32[]{:T(128)} %get-tuple-element.508, ...), kind=kOutput, calls=%fused_computation.8.clone.1 | convolution fusion | flops 1087373312 | bytes 22052868 | tf_op jit(solution)/shard_map/while/body/eval_jaxpr/kgrp,pkd->kgrd/dot_general | solution.py:26
  292.0 9.3 %bitcast_reduce_fusion.4 = (f32[4,4,256]{2,1,0:T(4,128)S(1)}, f32[4,1024,256,4]{2,1,3,0:T(8,128)}) fusion(bf16[256,4,4,128]{3,0,2,1:T(8,128)(2,1)S(1)} %get-tuple-element.521, bf16[2,1024,4,128]{3,1,2,0:T(8,128)(2,1)} %get-tuple-element.520, s32[]{:T(128)} %get-tuple-element.508), kind=kOutput, calls=%fused_computation.1.clone.1 | convolution fusion | flops 1082126336 | bytes 18891264 | tf_op jit(solution)/shard_map/while/body/eval_jaxpr/rkgd,pkd->kgrp/dot_general | solution.py:17
  301.3 8.7 %fusion.78 = f32[4,4,256]{2,1,0:T(4,128)S(1)} fusion(f32[4,1024,256,4]{2,1,3,0:T(8,128)} %get-tuple-element.444, f32[4,4,256]{2,1,0:T(4,128)S(1)} %max.16), kind=kLoop, calls=%fused_computation.4.clone.1 | loop fusion | flops 12578816 | bytes 16809984 | tf_op jit(solution)/shard_map/while/body/eval_jaxpr/reduce_sum | solution.py:25
  310.0 7.9 %multiply_add_fusion.5 = f32[4,4,256,128]{3,2,1,0:T(8,128)S(1)} fusion(f32[4,4,256,128]{3,2,1,0:T(8,128)S(1)} %get-tuple-element.511, f32[4,1024,256,4]{2,1,3,0:T(8,128)} %get-tuple-element.444, f32[4,4,256]{2,1,0:T(4,128)S(1)} %max.16, bf16[2,1024,4,128]{3,1,2,0:T(8,128)(2,1)S(1)} %copy-done.2, s32[]{:T(128)} %get-tuple-element.508, ...), kind=kOutput, calls=%fused_computation.8.clone.1 | convolution fusion | flops 1087373312 | bytes 22052868 | tf_op jit(solution)/shard_map/while/body/eval_jaxpr/kgrp,pkd->kgrd/dot_general | solution.py:26
  321.6 11.6 %convolution_convert_fusion = bf16[256,4096]{1,0:T(8,128)(2,1)} fusion(bf16[256,2048]{0,1:T(8,128)(2,1)S(1)} %bitcast.153, bf16[2048,4096]{1,0:T(8,128)(2,1)} %param.17), kind=kOutput, calls=%fused_computation.63 | convolution fusion | flops 4296015872 | bytes 19922944 | tf_op jit(solution)/shard_map/dot_general | solution.py:60
  333.3 30.7 %reduce-scatter.3.cloned.1.call-done = bf16[128,4096]{1,0:T(8,128)(2,1)} async-done(((bf16[256,4096]{1,0:T(8,128)(2,1)}), bf16[128,4096]{1,0:T(8,128)(2,1)}) %reduce-scatter.3.cloned.1.call-update) | async-done | bytes 1048592 | tf_op jit(solution)/shard_map/reduce_scatter | solution.py:111
  (91 shorter events, 123.8 us)
Async XLA Ops:
  7.2 56.2 %all-gather.7.cloned.1.call-start = ((), (), s32[]{:S(2)}) async-start(), calls=%async_computation.3 | async-start | bytes 4456448 | tf_op jit(solution)/shard_map/all_gather | solution.py:95
  7.9 130.5 %all-gather.5.cloned.1.call-start = ((), (), s32[]{:S(2)}) async-start(), calls=%async_computation.2 | async-start | bytes 8912896 | tf_op jit(solution)/shard_map/all_gather | solution.py:89
  8.6 324.6 %reduce-scatter.5.cloned.1.call-start = ((), (), s32[]{:S(2)}) async-start(), calls=%async_computation.5 | async-start | bytes 1572864 | tf_op jit(solution)/shard_map/reduce_scatter | solution.py:117
  88.4 5.8 %copy-start = (f32[4,1024,128,4]{2,1,3,0:T(8,128)S(1)}, f32[4,1024,128,4]{2,1,3,0:T(8,128)}, u32[]{:S(2)}) copy-start(f32[4,1024,128,4]{2,1,3,0:T(8,128)} %get-tuple-element.470) | copy-start | bytes 25165828 | tf_op jit(solution)/shard_map/while
  104.9 5.9 %copy-start = (f32[4,1024,128,4]{2,1,3,0:T(8,128)S(1)}, f32[4,1024,128,4]{2,1,3,0:T(8,128)}, u32[]{:S(2)}) copy-start(f32[4,1024,128,4]{2,1,3,0:T(8,128)} %get-tuple-element.470) | copy-start | bytes 25165828 | tf_op jit(solution)/shard_map/while
  128.9 235.0 %reduce-scatter.3.cloned.1.call-start = ((), (), s32[]{:S(2)}) async-start(), calls=%async_computation.4 | async-start | bytes 3145728 | tf_op jit(solution)/shard_map/reduce_scatter | solution.py:111
  168.2 8.7 %copy-start.1 = (bf16[1,1024,4,128]{3,2,1,0:T(4,128)(2,1)S(1)}, bf16[1,1024,4,128]{3,2,1,0:T(4,128)(2,1)}, u32[]{:S(2)}) copy-start(bf16[1,1024,4,128]{3,2,1,0:T(4,128)(2,1)} %get-tuple-element.458) | copy-start | bytes 3145732 | tf_op jit(solution)/shard_map/while
  195.2 8.7 %copy-start.1 = (bf16[1,1024,4,128]{3,2,1,0:T(4,128)(2,1)S(1)}, bf16[1,1024,4,128]{3,2,1,0:T(4,128)(2,1)}, u32[]{:S(2)}) copy-start(bf16[1,1024,4,128]{3,2,1,0:T(4,128)(2,1)} %get-tuple-element.458) | copy-start | bytes 3145732 | tf_op jit(solution)/shard_map/while
  222.1 8.7 %copy-start.1 = (bf16[1,1024,4,128]{3,2,1,0:T(4,128)(2,1)S(1)}, bf16[1,1024,4,128]{3,2,1,0:T(4,128)(2,1)}, u32[]{:S(2)}) copy-start(bf16[1,1024,4,128]{3,2,1,0:T(4,128)(2,1)} %get-tuple-element.458) | copy-start | bytes 3145732 | tf_op jit(solution)/shard_map/while
  249.1 8.7 %copy-start.1 = (bf16[1,1024,4,128]{3,2,1,0:T(4,128)(2,1)S(1)}, bf16[1,1024,4,128]{3,2,1,0:T(4,128)(2,1)}, u32[]{:S(2)}) copy-start(bf16[1,1024,4,128]{3,2,1,0:T(4,128)(2,1)} %get-tuple-element.458) | copy-start | bytes 3145732 | tf_op jit(solution)/shard_map/while
  275.3 8.7 %copy-start.2 = (bf16[2,1024,4,128]{3,1,2,0:T(8,128)(2,1)S(1)}, bf16[2,1024,4,128]{3,1,2,0:T(8,128)(2,1)}, u32[]{:S(2)}) copy-start(bf16[2,1024,4,128]{3,1,2,0:T(8,128)(2,1)} %get-tuple-element.522) | copy-start | bytes 6291460 | tf_op jit(solution)/shard_map/while
  301.3 8.7 %copy-start.2 = (bf16[2,1024,4,128]{3,1,2,0:T(8,128)(2,1)S(1)}, bf16[2,1024,4,128]{3,1,2,0:T(8,128)(2,1)}, u32[]{:S(2)}) copy-start(bf16[2,1024,4,128]{3,1,2,0:T(8,128)(2,1)} %get-tuple-element.522) | copy-start | bytes 6291460 | tf_op jit(solution)/shard_map/while
Sparse Core Ops, SparseCore 0:
  10.2 53.1 all-gather.6
  65.5 72.8 all-gather.4
  141.2 18.9 reduce-scatter.4
  333.4 30.5 reduce-scatter.2
where the time goes:
time: 372 us; the launch traced here: 370 us
  matrix products  136 us (37%)
  other arithmetic  67.1 us (18%)
  local copies, waits for them, and re-layouts  65 us (17%)
  waiting for transfers between devices  64.2 us (17%)
  blocking collectives  23.1 us (6%)
  between operations  13.9 us (4%)
    reduce_sum x8, other arithmetic, attend_block(): running_sum = running_sum * rescale + jnp.sum(shifted, axis=-1)  62.6 us
    dot_general x8, matrix products, attend_block(): jnp.einsum('rkgd,pkd->kgrp', grouped, key_block, preferred_element_type=j...  58.3 us
    dot_general x8, matrix products, attend_block(): jnp.einsum('kgrp,pkd->kgrd', shifted.astype(jnp.bfloat16), value_block, p...  57 us
    reduce_scatter x1, waiting for transfers between devices, per_device(): lax.psum_scatter(mix_rows(fine_attention, out_weight).astype(jnp.bfloat16...  30.7 us
    all_gather x1, blocking collectives, per_device(): lax.all_gather(coarse_levels.astype(jnp.bfloat16).reshape(1, -1), 'ctx',...  23.1 us
    all_gather x1, waiting for transfers between devices, per_device(): lax.all_gather(coarse_memory, 'ctx', axis=1, tiled=True)  22.8 us
    dot_general x2, matrix products, mix_rows(): return jnp.dot(attention, out_weight, preferred_element_type=jnp.float32)  21.1 us
    dynamic_slice x4, local copies, waits for them, and re-layouts, fold_keys(): result, unused = lax.scan(advance, running, (key_blocks, value_blocks))  12.9 us
  transfers between devices with their start and end apart: 4, of which 3 were waited for; matrix products, arithmetic and copies ran while one was open for 72% of the time, Pallas kernels for 0%

commit v1 on v0

v1 whole, which is shorter than its diff:
```python
import functools
import math

import jax
import jax.numpy as jnp
from jax import lax
from jax.experimental import pallas as pl
from jax.experimental.pallas import tpu as pltpu
from jax.sharding import PartitionSpec as P

HD = 128
MASKED = -1e30
LOG2E = math.log2(math.e)


def split_queries(rows):
    scaled = rows.astype(jnp.float32) * (HD ** (-0.5) * LOG2E)
    high = scaled.astype(jnp.bfloat16)
    low = (scaled - high.astype(jnp.float32)).astype(jnp.bfloat16)
    return jnp.concatenate([high, low], axis=1)


def scores_of(keys, pair):
    doubled = jnp.concatenate([keys, keys], axis=1)
    return lax.dot_general(
        doubled, pair, (((1,), (1,)), ((), ())), preferred_element_type=jnp.float32
    )


def fold(state, scores, values_t):
    highest, total, weighted = state
    new = jnp.maximum(highest, jnp.max(scores, axis=0, keepdims=True))
    rescale = jnp.exp2(highest - new)
    shifted = jnp.exp2(scores - new)
    total = total * rescale + jnp.sum(shifted, axis=0, keepdims=True)
    weighted = weighted * rescale + jnp.dot(
        values_t, shifted.astype(jnp.bfloat16), preferred_element_type=jnp.float32
    )
    return (new, total, weighted)


def start(columns):
    return (
        jnp.full((1, columns), MASKED, jnp.float32),
        jnp.zeros((1, columns), jnp.float32),
        jnp.zeros((HD, columns), jnp.float32),
    )


def attention_kernel(
    ratio, span, fq_ref, fkv_ref, cq_ref, ckv_ref, qlev_ref, klev_ref, fo_ref, co_ref, vt_ref
):
    fine_keys, coarse_keys = fkv_ref.shape[1], ckv_ref.shape[1]
    rows, coarse_rows = fq_ref.shape[0], cq_ref.shape[0]
    chunks = [(ckv_ref, at, at) for at in range(0, coarse_keys, span)]
    coarse_count = len(chunks)
    chunks += [(fkv_ref, at, coarse_keys + at) for at in range(0, fine_keys, span)]
    for ref, at, to in chunks:
        vt_ref[:, to : to + span] = ref[1, at : at + span, :].T

    def run(pair, count, allowed):
        state = start(pair.shape[0])

        def scored(which):
            ref, at, to = chunks[which]
            scores = scores_of(ref[0, at : at + span, :], pair)
            return allowed(scores, at)

        ahead = scored(0)
        for which in range(count):
            scores = ahead
            if which + 1 < count:
                ahead = scored(which + 1)
            to = chunks[which][2]
            state = fold(state, scores, vt_ref[:, to : to + span])
        return (state[2] / state[1]).T.astype(jnp.bfloat16)

    @pl.loop(0, ratio)
    def _(head):
        columns = pl.ds(pl.multiple_of(head * HD, HD), HD)
        fo_ref[:, columns] = run(
            split_queries(fq_ref[:, columns]), len(chunks), lambda scores, at: scores
        )

    stack = 2 if ratio % 2 == 0 else 1
    levels = jnp.concatenate([qlev_ref[...]] * stack, axis=1)

    def masked(scores, at):
        return jnp.where(klev_ref[at : at + span, :] <= levels, scores, MASKED)

    @pl.loop(0, ratio // stack)
    def _(part):
        heads = [
            pl.ds(pl.multiple_of((part * stack + i) * HD, HD), HD) for i in range(stack)
        ]
        pair = jnp.concatenate([split_queries(cq_ref[:, columns]) for columns in heads], axis=0)
        result = run(pair, coarse_count, masked)
        for i, columns in enumerate(heads):
            co_ref[:, columns] = result[i * coarse_rows : (i + 1) * coarse_rows]


def attention(fine_query, fine_kv, coarse_query, coarse_kv, query_levels, key_levels):
    groups = fine_kv.shape[2] // HD
    width = fine_query.shape[1] // groups
    ratio = width // HD
    rows, coarse_rows = fine_query.shape[0], coarse_query.shape[0]
    fine_keys, coarse_keys = fine_kv.shape[1], coarse_kv.shape[1]
    span = math.gcd(math.gcd(fine_keys, coarse_keys), 512)
    return pl.pallas_call(
        functools.partial(attention_kernel, ratio, span),
        grid=(groups,),
        out_shape=(
            jax.ShapeDtypeStruct(fine_query.shape, jnp.bfloat16),
            jax.ShapeDtypeStruct(coarse_query.shape, jnp.bfloat16),
        ),
        in_specs=[
            pl.BlockSpec((rows, width), lambda g: (0, g)),
            pl.BlockSpec((2, fine_keys, HD), lambda g: (0, 0, g)),
            pl.BlockSpec((coarse_rows, width), lambda g: (0, g)),
            pl.BlockSpec((2, coarse_keys, HD), lambda g: (0, 0, g)),
            pl.BlockSpec((1, coarse_rows), lambda g: (0, 0)),
            pl.BlockSpec((coarse_keys, 1), lambda g: (0, 0)),
        ],
        out_specs=(
            pl.BlockSpec((rows, width), lambda g: (0, g)),
            pl.BlockSpec((coarse_rows, width), lambda g: (0, g)),
        ),
        scratch_shapes=[pltpu.VMEM((HD, fine_keys + coarse_keys), jnp.bfloat16)],
        compiler_params=pltpu.CompilerParams(vmem_limit_bytes=50 << 20),
    )(fine_query, fine_kv, coarse_query, coarse_kv, query_levels, key_levels)


def per_device(fine_query, fine_memory, coarse_query, coarse_memory, coarse_scale, out_weight):
    levels = coarse_scale.astype(jnp.float32)
    key_levels = lax.all_gather(
        levels.astype(jnp.bfloat16).reshape(1, -1), "ctx", axis=1, tiled=True
    )
    coarse_kv = lax.all_gather(coarse_memory, "ctx", axis=1, tiled=True)
    fine_kv = lax.all_gather(fine_memory, "ctx", axis=1, tiled=True)
    fine_attention, coarse_attention = attention(
        fine_query,
        fine_kv,
        coarse_query,
        coarse_kv,
        levels.reshape(1, -1),
        key_levels.astype(jnp.float32).reshape(-1, 1),
    )

    def mix(rows):
        partial = jnp.dot(rows, out_weight, preferred_element_type=jnp.float32)
        return lax.psum_scatter(
            partial.astype(jnp.bfloat16), "head", scatter_dimension=0, tiled=True
        )

    return (mix(fine_attention), mix(coarse_attention))


def solution(mesh):
    placed = (
        P("ctx", "head"),
        P(None, "ctx", "head"),
        P("ctx", "head"),
        P(None, "ctx", "head"),
        P("ctx"),
        P("head", None),
    )
    return jax.shard_map(
        per_device,
        mesh=mesh,
        in_specs=placed,
        out_specs=(P(("ctx", "head"), None), P(("ctx", "head"), None)),
        check_vma=False,
    )
```

time: 372 us -> 270 us (0.73)
  matrix products: 136 us -> 21 us
  waiting for transfers between devices: 64.2 us -> 148 us
  other arithmetic: 67.1 us -> 0.66 us
  local copies, waits for them, and re-layouts: 65 us -> 3.61 us
  Pallas kernels: 0 us -> 59.7 us
    dot_general x18 -> x2, matrix products: 136 us -> 21 us  [mix(): partial = jnp.dot(rows, out_weight, preferred_element_type=jnp.float32)]
    all_gather x2, waiting for transfers between devices: 32.1 us -> 105 us  [the longest x1 75.1 us: per_device(): fine_kv = lax.all_gather(fine_memory, 'ctx', axis=1, tiled=True)]
    reduce_sum x8 -> x0, other arithmetic: 62.6 us -> none  [attend_block(): running_sum = running_sum * rescale + jnp.sum(shifted, axis=-1)]
    pallas_call x0 -> x1, Pallas kernels: none -> 59.7 us  [attention(): pl.pallas_call(functools.partial(attention_kernel, ratio, span), grid=(gr...]
    another operation x4 -> x0, local copies, waits for them, and re-layouts: 21.9 us -> none  [the longest x2 10.9 us: fold_keys(): key_blocks = kv_piece[0].reshape(block_count, span_rows, groups, -1)]
    dynamic_slice x6 -> x0, local copies, waits for them, and re-layouts: 12.9 us -> none  [the longest x4 12.9 us: fold_keys(): result, unused = lax.scan(advance, running, (key_blocks, value_blocks))]
    while x28 -> x0, local copies, waits for them, and re-layouts: 12 us -> none  [the longest x3 8.34 us: fold_keys(): result, unused = lax.scan(advance, running, (key_blocks, value_blocks))]
    reduce_scatter x2, waiting for transfers between devices: 30.7 us -> 41.8 us  [mix(): lax.psum_scatter(partial.astype(jnp.bfloat16), 'head', scatter_dimension=...]
  transfers between devices with their start and end apart: 4 -> 4, of which waited for: 3 -> 4; matrix products, arithmetic and copies ran while one was open for 72% -> 5% of each run, Pallas kernels for 0% -> 0%
where the time goes in v1:
time: 270 us
  waiting for transfers between devices  148 us (55%)
  Pallas kernels  59.7 us (22%)
  blocking collectives  23.1 us (9%)
  matrix products  21 us (8%)
  between operations  13.8 us (5%)
  local copies, waits for them, and re-layouts  3.61 us (1%)
    all_gather x1, waiting for transfers between devices, per_device(): fine_kv = lax.all_gather(fine_memory, 'ctx', axis=1, tiled=True)  75.1 us
    pallas_call x1, Pallas kernels, attention(): pl.pallas_call(functools.partial(attention_kernel, ratio, span), grid=(gr...  59.7 us
    reduce_scatter x2, waiting for transfers between devices, mix(): lax.psum_scatter(partial.astype(jnp.bfloat16), 'head', scatter_dimension=...  41.8 us
    all_gather x1, waiting for transfers between devices, per_device(): coarse_kv = lax.all_gather(coarse_memory, 'ctx', axis=1, tiled=True)  29.6 us
    all_gather x1, blocking collectives, per_device(): lax.all_gather(levels.astype(jnp.bfloat16).reshape(1, -1), 'ctx', axis=1,...  23.1 us
    dot_general x2, matrix products, mix(): partial = jnp.dot(rows, out_weight, preferred_element_type=jnp.float32)  21 us
  transfers between devices with their start and end apart: 4, of which 4 were waited for; matrix products, arithmetic and copies ran while one was open for 5% of the time, Pallas kernels for 0%

profile of v1, /device:TPU:0, one launch (start us, length us, event | category | flops | bytes accessed | tf_op | source)
XLA Modules:
  0.0 269.8 jit_solution(2942692101883727852)
XLA Ops:
  7.2 0.0 all-gather.7.cloned.1.call-start
  7.2 0.7 all-gather.7.cloned.1.call-update
  7.9 0.0 all-gather.5.cloned.1.call-start
  7.9 0.7 all-gather.5.cloned.1.call-update
  8.6 0.0 reduce-scatter.5.cloned.1.call-start
  8.7 0.7 convert_bitcast_fusion
  9.4 23.1 %all-gather.1 = bf16[16,1,128]{2,1,0:T(2,128)(2,1)S(1)} all-gather(bf16[1,1,128]{2,1,0:T(2,128)(2,1)S(1)} %get-tuple-element.6), channel_id=2, replica_groups=mesh['ctx'=16,'head'=2] {'ctx'}, dimensions={0}, use_global_device_ids=true | all-gather | bytes 4352 | tf_op jit(solution)/shard_map/all_gather | solution.py:135
  32.5 1.3 copy.10.klev_ref
  33.8 29.6 %all-gather.7.cloned.1.call-done.ckv_ref = bf16[2,2048,512]{2,1,0:T(8,128)(2,1)} async-done(((bf16[2,128,512]{2,1,0:T(8,128)(2,1)}), bf16[2,2048,512]{2,1,0:T(8,128)(2,1)}) %all-gather.7.cloned.1.call-update) | async-done | bytes 4194320 | tf_op jit(solution)/shard_map/all_gather | solution.py:138
  63.4 75.1 %all-gather.5.cloned.1.call-done.fkv_ref = bf16[2,4096,512]{2,1,0:T(8,128)(2,1)} async-done(((bf16[2,256,512]{2,1,0:T(8,128)(2,1)}), bf16[2,4096,512]{2,1,0:T(8,128)(2,1)}) %all-gather.5.cloned.1.call-update) | async-done | bytes 8388624 | tf_op jit(solution)/shard_map/all_gather | solution.py:139
  138.4 0.0 copy-start
  138.4 1.2 copy-done
  139.7 0.0 copy-start.1
  139.7 1.0 copy-done.1
  140.7 59.7 %shard_map.77 = (bf16[256,2048]{1,0:T(8,128)(2,1)S(1)}, bf16[128,2048]{1,0:T(8,128)(2,1)S(1)}) custom-call(bf16[256,2048]{1,0:T(8,128)(2,1)S(1)} %copy-done, bf16[2,4096,512]{2,1,0:T(8,128)(2,1)} %all-gather.5.cloned.1.call-done.fkv_ref, bf16[128,2048]{1,0:T(8,128)(2,1)S(1)} %copy-done.1, bf16[2,2048,512]{2,1,0:T(8,128)(2,1)} %all-gather.7.cloned.1.call-done.ckv_ref, ...), custom_call_target="tpu_custom_call" | custom-call | tf_op jit(solution)/shard_map/pallas_call | solution.py:109
  200.5 9.1 %convolution_convert_fusion.1 = bf16[128,4096]{1,0:T(8,128)(2,1)} fusion(bf16[128,2048]{1,0:T(8,128)(2,1)S(1)} %get-tuple-element.5, bf16[2048,4096]{1,0:T(8,128)(2,1)} %param.11), kind=kOutput, calls=%fused_computation.1 | convolution fusion | flops 2148007936 | bytes 18350080 | tf_op jit(solution)/shard_map/dot_general | solution.py:150
  209.6 0.0 reduce-scatter.5.cloned.1.call-update
  209.6 0.0 reduce-scatter.3.cloned.1.call-start
  209.6 11.9 %convolution_convert_fusion = bf16[256,4096]{1,0:T(8,128)(2,1)} fusion(bf16[256,2048]{1,0:T(8,128)(2,1)S(1)} %get-tuple-element.4, bf16[2048,4096]{1,0:T(8,128)(2,1)} %param.11), kind=kOutput, calls=%fused_computation | convolution fusion | flops 4296015872 | bytes 19922944 | tf_op jit(solution)/shard_map/dot_general | solution.py:150
  221.5 0.0 reduce-scatter.3.cloned.1.call-update
  221.5 7.2 %reduce-scatter.5.cloned.1.call-done = bf16[64,4096]{1,0:T(8,128)(2,1)} async-done(((bf16[128,4096]{1,0:T(8,128)(2,1)}), bf16[64,4096]{1,0:T(8,128)(2,1)}) %reduce-scatter.5.cloned.1.call-update) | async-done | bytes 524304 | tf_op jit(solution)/shard_map/reduce_scatter | solution.py:151
  228.7 34.6 %reduce-scatter.3.cloned.1.call-done = bf16[128,4096]{1,0:T(8,128)(2,1)} async-done(((bf16[256,4096]{1,0:T(8,128)(2,1)}), bf16[128,4096]{1,0:T(8,128)(2,1)}) %reduce-scatter.3.cloned.1.call-update) | async-done | bytes 1048592 | tf_op jit(solution)/shard_map/reduce_scatter | solution.py:151
  (1 shorter events, 0.0 us)
Async XLA Ops:
  7.2 56.2 %all-gather.7.cloned.1.call-start = ((), (), s32[]{:S(2)}) async-start(), calls=%async_computation.3 | async-start | bytes 4456448 | tf_op jit(solution)/shard_map/all_gather | solution.py:138
  7.9 130.5 %all-gather.5.cloned.1.call-start = ((), (), s32[]{:S(2)}) async-start(), calls=%async_computation.2 | async-start | bytes 8912896 | tf_op jit(solution)/shard_map/all_gather | solution.py:139
  8.6 220.1 %reduce-scatter.5.cloned.1.call-start = ((), (), s32[]{:S(2)}) async-start(), calls=%async_computation.5 | async-start | bytes 1572864 | tf_op jit(solution)/shard_map/reduce_scatter | solution.py:151
  138.4 1.2 copy-start
  139.7 1.0 copy-start.1
  209.6 53.7 %reduce-scatter.3.cloned.1.call-start = ((), (), s32[]{:S(2)}) async-start(), calls=%async_computation.4 | async-start | bytes 3145728 | tf_op jit(solution)/shard_map/reduce_scatter | solution.py:151
Sparse Core Ops, SparseCore 0:
  10.2 53.1 all-gather.6
  65.6 72.8 all-gather.4
  209.7 18.9 reduce-scatter.4
  231.4 31.8 reduce-scatter.2
